TPU v7x, 256 devices: a whole 4x4x8 slice. The times are simulated.
256 devices in a mesh: ctx: 64 (over y, z, core), vocab: 4 (over x).
Axes of the slice: x: 4, y: 4, z: 8, core: 2. Of those that a mesh axis runs over, the one named last changes fastest.
Arguments:
- hidden_states: bfloat16 [16384, 8192], P('ctx'), may hold values from -24 to 24
- master: float32 [1024, 8192], P(('vocab', 'ctx')), may hold values from -1 to 1
- moment: float32 [1024, 8192], P(('vocab', 'ctx')), may hold values from -6 to 6
- second: float32 [1024, 8192], P(('vocab', 'ctx')), may hold values from 0.05 to 5
- targets: int32 [16384], P('ctx'), may hold values from 0 to 2047, as said below
- loss_mask: int32 [16384], P('ctx'), may hold values from 0 to 1, as said below
- prior_lse: float32 [16384], P('ctx'), may hold values from 6 to 9
- prior_target: float32 [16384], P('ctx'), may hold values from -5 to 5
- span_order: int32 [128], replicated, may hold values from 0 to 127, as said below
Outputs:
- token_loss: float32 [16384], P('ctx')
- mean_loss: float32 [], replicated
- hidden_grad: bfloat16 [16384, 8192], P('ctx', 'vocab')
- new_master: float32 [1024, 8192], P(('vocab', 'ctx'))
- new_moment: float32 [1024, 8192], P(('vocab', 'ctx'))
- new_second: float32 [1024, 8192], P(('vocab', 'ctx'))
Inputs may be any that keep to these rules, and one draw needn't show every extreme that they name: `targets`: ids of 1024 and more fall in this block, id minus 1024 naming its row; smaller ids lie in earlier blocks. `loss_mask`: 1 on a leading run of the slab's positions and 0 after it; at least 4096 ones. `span_order`: each span number once.
All inputs are finite; a program needn't handle non-finite values.
Results may differ from a plain program's by a relative error of at most 0.0085.
Values may be sent and summed in bfloat16 or wider, within the bound.
No kernel may reach another device: no remote copies, remote signals or barrier semaphores. Data moves between devices by JAX's collectives and lax.ppermute only.
A program may use at most 128 MiB of HBM per device.

v0:
```python
import jax
import jax.numpy as jnp
from jax import lax
from jax.sharding import PartitionSpec as P

loss_scale = 1048576.0
clip_norm = 0.004
beta_one = 0.9
beta_two = 0.95
learn_rate = 0.001
weight_decay = 0.1
adam_eps = 1e-08


def project(block_rows, weight_rows):
    return lax.dot_general(
        block_rows, weight_rows, (((1,), (1,)), ((), ())), preferred_element_type=jnp.float32
    )


def body(
    hidden_states, master, moment, second, targets, loss_mask, prior_lse, prior_target, span_order
):
    tok_rows, feat_dim = hidden_states.shape
    shard_rows = master.shape[0]
    ctx_count = lax.axis_size("ctx")
    vocab_count = lax.axis_size("vocab")
    ctx_place = lax.axis_index("ctx")
    vocab_place = lax.axis_index("vocab")
    half_rows = tok_rows // 2
    group_rows = shard_rows * ctx_count
    block_total = group_rows * vocab_count
    head_rows = master.astype(jnp.bfloat16)
    all_targets, all_mask, all_prior, all_outside = (
        lax.all_gather(targets, "ctx", axis=0, tiled=True),
        lax.all_gather(loss_mask, "ctx", axis=0, tiled=True),
        lax.all_gather(prior_lse, "ctx", axis=0, tiled=True),
        lax.all_gather(prior_target, "ctx", axis=0, tiled=True),
    )

    def own_rows(whole):
        pieces = [
            lax.dynamic_slice_in_dim(
                whole, span_order[2 * ctx_place + offset] * half_rows, half_rows, 0
            )
            for offset in (0, 1)
        ]
        return jnp.concatenate(pieces, 0)

    tgt_rows = own_rows(all_targets)
    mask_rows = own_rows(all_mask).astype(jnp.float32)
    prior_rows = own_rows(all_prior)
    outside = own_rows(all_outside)
    local_col = tgt_rows - block_total - vocab_place * group_rows
    token_count = jnp.sum(all_mask.astype(jnp.float32))

    def hit_table(col_count):
        columns = jnp.arange(col_count, dtype=jnp.int32)
        return columns[None, :] == local_col[:, None]

    gathered = lax.all_gather(head_rows, "ctx", axis=0, tiled=True)
    logits = project(hidden_states, gathered)
    top_local = jnp.maximum(prior_rows, jnp.max(logits, axis=1))
    sum_local = jnp.sum(jnp.exp(logits - top_local[:, None]), axis=1)
    target_local = jnp.sum(jnp.where(hit_table(group_rows), logits, 0.0), axis=1)
    top_value = lax.pmax(top_local, "vocab")
    sum_total, target_sum = lax.psum(
        (sum_local * jnp.exp(top_local - top_value), target_local), "vocab"
    )
    log_total = top_value + jnp.log(jnp.exp(prior_rows - top_value) + sum_total)
    target_logit = jnp.where(tgt_rows >= block_total, target_sum, outside)
    loss_rows = mask_rows * (log_total - target_logit)
    grad_scale = loss_scale / token_count
    onehot = hit_table(group_rows).astype(jnp.float32)
    dlogits = (
        mask_rows[:, None] * (jnp.exp(logits - log_total[:, None]) - onehot) * grad_scale
    ).astype(jnp.bfloat16)
    columns = dlogits
    row_grad = lax.psum_scatter(
        lax.dot_general(
            columns, hidden_states, (((0,), (0,)), ((), ())), preferred_element_type=jnp.float32
        ),
        "ctx",
        scatter_dimension=0,
        tiled=True,
    )
    partial_value = jnp.dot(dlogits, gathered, preferred_element_type=jnp.float32)
    hidden_grad = lax.psum_scatter(
        partial_value.astype(jnp.bfloat16), "vocab", scatter_dimension=1, tiled=True
    )
    all_losses = lax.all_gather(loss_rows, "ctx", axis=0, tiled=True)
    mean_loss = jnp.sum(all_losses) / token_count
    slot_ids = jnp.arange(span_order.shape[0], dtype=jnp.int32)
    natural = []
    for offset in (0, 1):
        span_id = 2 * ctx_place + offset
        slot_place = jnp.sum(jnp.where(span_order == span_id, slot_ids, 0))
        natural.append(lax.dynamic_slice_in_dim(all_losses, slot_place * half_rows, half_rows, 0))
    token_loss = jnp.concatenate(natural, 0)
    square_sum = lax.psum(jnp.sum(row_grad * row_grad), ("ctx", "vocab"))
    norm_value = jnp.sqrt(square_sum) / loss_scale
    clip_factor = jnp.minimum(1.0, clip_norm / (norm_value + 1e-06))
    clipped = row_grad * clip_factor
    new_moment = beta_one * moment + (1.0 - beta_one) * clipped
    new_second = beta_two * second + (1.0 - beta_two) * clipped * clipped
    new_master = master - learn_rate * (
        new_moment / (jnp.sqrt(new_second) + adam_eps) + weight_decay * master
    )
    return (token_loss, mean_loss, hidden_grad, new_master, new_moment, new_second)


def solution(mesh):
    in_specs = (
        P("ctx", None),
        P(("vocab", "ctx"), None),
        P(("vocab", "ctx"), None),
        P(("vocab", "ctx"), None),
        P("ctx"),
        P("ctx"),
        P("ctx"),
        P("ctx"),
        P(),
    )
    out_specs = (
        P("ctx"),
        P(),
        P("ctx", "vocab"),
        P(("vocab", "ctx"), None),
        P(("vocab", "ctx"), None),
        P(("vocab", "ctx"), None),
    )
    return jax.shard_map(body, mesh=mesh, in_specs=in_specs, out_specs=out_specs, check_vma=False)
```

profile of v0, /device:TPU:1, one launch (start us, length us, event | category | flops | bytes accessed | tf_op | source)
XLA Modules:
  0.0 517.7 jit_solution(13695655698217705344)
XLA Ops:
  7.2 1.6 convert_bitcast_fusion
  8.9 1.3 fusion.13
  11.5 48.5 %all-gather = s32[64,1,256]{2,1,0:T(1,128)S(1)} all-gather(s32[1,1,256]{2,1,0:T(1,128)} %bitcast.26), channel_id=1, replica_groups=mesh['ctx'=64,'vocab'=4] {'ctx'}, dimensions={0}, use_global_device_ids=true | all-gather | bytes 66560 | tf_op jit(solution)/shard_map/all_gather | solution.py:36
  60.0 0.6 convert_reduce_fusion
  61.3 42.9 %all-gather.3 = s32[64,1,256]{2,1,0:T(1,128)S(1)} all-gather(s32[1,1,256]{2,1,0:T(1,128)} %bitcast.27), channel_id=1, replica_groups=mesh['ctx'=64,'vocab'=4] {'ctx'}, dimensions={0}, use_global_device_ids=true | all-gather | bytes 66560 | tf_op jit(solution)/shard_map/all_gather | solution.py:35
  104.2 41.5 %all-gather.1 = f32[64,1,256]{2,1,0:T(1,128)S(1)} all-gather(f32[1,1,256]{2,1,0:T(1,128)} %bitcast.28), channel_id=1, replica_groups=mesh['ctx'=64,'vocab'=4] {'ctx'}, dimensions={0}, use_global_device_ids=true | all-gather | bytes 66560 | tf_op jit(solution)/shard_map/all_gather | solution.py:37
  145.7 42.8 %all-gather.4 = f32[64,1,256]{2,1,0:T(1,128)S(1)} all-gather(f32[1,1,256]{2,1,0:T(1,128)} %bitcast.29), channel_id=1, replica_groups=mesh['ctx'=64,'vocab'=4] {'ctx'}, dimensions={0}, use_global_device_ids=true | all-gather | bytes 66560 | tf_op jit(solution)/shard_map/all_gather | solution.py:38
  188.8 6.9 %reshape.70 = bf16[256,8192]{1,0:T(8,128)(2,1)} reshape(bf16[64,4,8192]{2,1,0:T(4,128)(2,1)} %all-gather.8.cloned.1.call-done) | data formatting | bytes 8388608
  195.7 4.8 fusion.14
  200.5 8.5 %pmax.7 = f32[256]{0:T(256)S(1)} all-reduce(f32[256]{0:T(256)S(1)} %fusion.5), channel_id=1, replica_groups=mesh['ctx'=64,'vocab'=4] {'vocab'}, use_global_device_ids=true, to_apply=%region_1.0 | all-reduce | flops 256 | bytes 2048 | tf_op jit(solution)/shard_map/pmax | solution.py:66
  209.0 0.1 select_reduce_fusion
  209.1 6.0 %all-reduce.1 = (f32[256]{0:T(256)S(1)}, f32[256]{0:T(256)S(1)}) all-reduce(f32[256]{0:T(256)S(1)} %exponential_multiply_fusion, f32[256]{0:T(256)S(1)} %get-tuple-element.6), channel_id=1, replica_groups=mesh['ctx'=64,'vocab'=4] {'vocab'}, use_global_device_ids=true, to_apply=%region_3.4 | all-reduce | flops 512 | bytes 4096 | tf_op jit(solution)/shard_map/psum | solution.py:67
  215.1 6.7 %fusion.6 = f32[256,8192]{1,0:T(8,128)} fusion(bf16[256,8192]{1,0:T(8,128)(2,1)} %param.9, f32[256,256]{0,1:T(8,128)S(1)} %get-tuple-element.30, f32[]{:T(128)S(6)} %div.16, f32[256]{0:T(256)S(1)} %get-tuple-element.16, f32[256]{0:T(256)S(1)} %add_convert_fusion, s32[256]{0:T(256)S(1)} %add_subtract_fusion), kind=kOutput, calls=%fused_computation.27 | convolution fusion | flops 1074200576 | bytes 12848132 | tf_op jit(solution)/shard_map/dot_general | solution.py:80
  221.9 5.5 %convolution_convert_fusion = bf16[256,8192]{1,0:T(8,128)(2,1)} fusion(bf16[256,8192]{1,0:T(8,128)(2,1)} %reshape.70, f32[256,256]{0,1:T(8,128)S(1)} %get-tuple-element.30, f32[]{:T(128)S(6)} %div.16, f32[256]{0:T(256)S(1)} %get-tuple-element.16, f32[256]{0:T(256)S(1)} %add_convert_fusion, s32[256]{0:T(256)S(1)} %add_subtract_fusion), kind=kOutput, calls=%fused_computation | convolution fusion | flops 1076297728 | bytes 8653828 | tf_op jit(solution)/shard_map/dot_general | solution.py:87
  227.4 0.6 copy-done.3
  228.0 0.6 fusion.3
  230.0 0.6 dynamic-slice
  231.2 45.4 %all-gather.5 = f32[64,1,256]{2,1,0:T(1,128)S(1)} all-gather(f32[1,1,256]{2,1,0:T(1,128)S(1)} %bitcast.25), channel_id=1, replica_groups=mesh['ctx'=64,'vocab'=4] {'ctx'}, dimensions={0}, use_global_device_ids=true | all-gather | bytes 66560 | tf_op jit(solution)/shard_map/all_gather | solution.py:91
  276.6 0.7 reduce_sum.67
  277.4 0.6 pad_maximum_fusion.1
  278.0 147.5 %all-reduce.4.cloned.1.call-done = f32[256,8192]{1,0:T(8,128)} async-done(((f32[256,8192]{1,0:T(8,128)}), f32[256,8192]{1,0:T(8,128)}) %all-reduce.4.cloned.1.call-update) | async-done | bytes 8388624
  425.5 1.6 multiply_reduce_fusion
  428.4 79.0 %psum.23 = f32[]{:T(128)} all-reduce(f32[]{:T(128)} %multiply_reduce_fusion), channel_id=1, replica_groups=mesh['ctx'=64,'vocab'=4] {'ctx','vocab'}, use_global_device_ids=true, to_apply=%region_13.14 | all-reduce | flops 1 | bytes 8 | tf_op jit(solution)/shard_map/psum | solution.py:100
  508.1 1.9 multiply_subtract_fusion
  (27 shorter events, 0.6 us)
Async XLA Ops:
  7.2 181.6 %all-gather.8.cloned.1.call-start = ((), (), s32[]{:S(2)}) async-start(), calls=%async_computation.2 | async-start | bytes 4259840 | tf_op jit(solution)/shard_map/all_gather | solution.py:61
  8.8 416.7 %all-reduce.4.cloned.1.call-start = ((), (), s32[]{:S(2)}) async-start(), calls=%async_computation.3 | async-start | bytes 16777216
  221.8 288.2 %reduce-scatter.2.cloned.1.call-start = ((), (), s32[]{:S(2)}) async-start(), calls=%async_computation.1 | async-start | bytes 5242880 | tf_op jit(solution)/shard_map/reduce_scatter | solution.py:88
  227.3 0.7 copy-start.3
  227.4 2.6 copy-start.4
  227.4 280.8 %copy-start = (f32[4,8192]{1,0:T(4,128)S(1)}, f32[4,8192]{1,0:T(4,128)}, u32[]{:S(2)}) copy-start(f32[4,8192]{1,0:T(4,128)} %param.10) | copy-start | bytes 393220
  227.4 280.8 %copy-start.1 = (f32[4,8192]{1,0:T(4,128)S(1)}, f32[4,8192]{1,0:T(4,128)}, u32[]{:S(2)}) copy-start(f32[4,8192]{1,0:T(4,128)} %param.12) | copy-start | bytes 393220
  227.4 280.8 %copy-start.2 = (f32[4,8192]{1,0:T(4,128)S(1)}, f32[4,8192]{1,0:T(4,128)}, u32[]{:S(2)}) copy-start(f32[4,8192]{1,0:T(4,128)} %param.11) | copy-start | bytes 393220
Sparse Core Ops, SparseCore 0:
  11.3 83.5 all-gather.7
  221.9 203.4 all-reduce.3
  428.6 50.3 reduce-scatter.1
where the time goes:
time: 518 us
  blocking collectives  314 us (61%)
  waiting for transfers between devices  148 us (29%)
  between operations  21 us (4%)
  matrix products  16.9 us (3%)
  local copies, waits for them, and re-layouts  9.84 us (2%)
  other arithmetic  7.74 us (1%)
    unnamed x4, waiting for transfers between devices  148 us
    psum x1, blocking collectives, body(): square_sum = lax.psum(jnp.sum(row_grad * row_grad), ('ctx', 'vocab'))  79 us
    all_gather x1, blocking collectives, body(): lax.all_gather(loss_mask, 'ctx', axis=0, tiled=True)  48.5 us
    all_gather x1, blocking collectives, body(): all_losses = lax.all_gather(loss_rows, 'ctx', axis=0, tiled=True)  45.4 us
    all_gather x1, blocking collectives, body(): lax.all_gather(targets, 'ctx', axis=0, tiled=True)  42.9 us
    all_gather x1, blocking collectives, body(): lax.all_gather(prior_target, 'ctx', axis=0, tiled=True)  42.8 us
    all_gather x1, blocking collectives, body(): lax.all_gather(prior_lse, 'ctx', axis=0, tiled=True)  41.5 us
  transfers between devices with their start and end apart: 3, of which 1 were waited for; matrix products, arithmetic and copies ran while one was open for 3% of the time, Pallas kernels for 0%

commit v1 on v0

--- a/solution.py
+++ b/solution.py
@@ -31,11 +31,15 @@
     group_rows = shard_rows * ctx_count
     block_total = group_rows * vocab_count
     head_rows = master.astype(jnp.bfloat16)
+    link_the_cubes = lambda original, named_axis, dim_i: jnp.concatenate(
+        lax.all_to_all(jnp.stack(lax.psum(1, named_axis) * [original]), named_axis, 0, 0),
+        axis=dim_i,
+    )
     all_targets, all_mask, all_prior, all_outside = (
         lax.all_gather(targets, "ctx", axis=0, tiled=True),
         lax.all_gather(loss_mask, "ctx", axis=0, tiled=True),
         lax.all_gather(prior_lse, "ctx", axis=0, tiled=True),
-        lax.all_gather(prior_target, "ctx", axis=0, tiled=True),
+        link_the_cubes(prior_target, "ctx", 0),
     )
 
     def own_rows(whole):

time: 518 us -> 487 us (0.940)
  blocking collectives: 314 us -> 269 us
  starting transfers between devices: 0.12 us -> 13.3 us
    all_gather x1 -> x0, blocking collectives: 42.8 us -> none  [body(): lax.all_gather(prior_target, 'ctx', axis=0, tiled=True)]
    all_to_all x0 -> x1, starting transfers between devices: none -> 13.1 us  [body(): lax.all_to_all(jnp.stack(lax.psum(1, named_axis) * [original]), named_axi...]
    all_gather x1, blocking collectives: 48.5 us -> 42 us  [body(): lax.all_gather(loss_mask, 'ctx', axis=0, tiled=True)]
  transfers between devices with their start and end apart: 3 -> 4, of which waited for: 1 -> 1; matrix products, arithmetic and copies ran while one was open for 3% -> 3% of each run, Pallas kernels for 0% -> 0%
where the time goes in v1:
time: 487 us
  blocking collectives  269 us (55%)
  waiting for transfers between devices  148 us (30%)
  between operations  21 us (4%)
  matrix products  16.9 us (3%)
  starting transfers between devices  13.3 us (3%)
  local copies, waits for them, and re-layouts  11.2 us (2%)
  other arithmetic  7.74 us (2%)
    unnamed x4, waiting for transfers between devices  148 us
    psum x1, blocking collectives, body(): square_sum = lax.psum(jnp.sum(row_grad * row_grad), ('ctx', 'vocab'))  79 us
    all_gather x1, blocking collectives, body(): all_losses = lax.all_gather(loss_rows, 'ctx', axis=0, tiled=True)  46.1 us
    all_gather x1, blocking collectives, body(): lax.all_gather(targets, 'ctx', axis=0, tiled=True)  44.8 us
    all_gather x1, blocking collectives, body(): lax.all_gather(prior_lse, 'ctx', axis=0, tiled=True)  42.3 us
    all_gather x1, blocking collectives, body(): lax.all_gather(loss_mask, 'ctx', axis=0, tiled=True)  42 us
    all_to_all x1, starting transfers between devices, body(): lax.all_to_all(jnp.stack(lax.psum(1, named_axis) * [original]), named_axi...  13.1 us
  transfers between devices with their start and end apart: 4, of which 1 were waited for; matrix products, arithmetic and copies ran while one was open for 3% of the time, Pallas kernels for 0%

profile of v1, /device:TPU:1, one launch (start us, length us, event | category | flops | bytes accessed | tf_op | source)
XLA Modules:
  0.0 486.5 jit_solution(11996375318012450111)
XLA Ops:
  7.2 1.6 convert_bitcast_fusion
  8.8 1.3 stack.2
  10.1 13.1 %all-to-all-start = ((f32[64,1,256]{2,1,0:T(1,128)}), f32[64,1,256]{2,1,0:T(1,128)S(1)}, u32[]{:S(2)}, u32[]{:S(2)}) async-start(f32[64,1,256]{2,1,0:T(1,128)} %stack.2), calls=%async_computation | async-start | bytes 131072 | tf_op jit(solution)/shard_map/all_to_all | solution.py:35
  23.3 1.3 fusion.13
  26.0 44.8 %all-gather.3 = s32[64,1,256]{2,1,0:T(1,128)S(1)} all-gather(s32[1,1,256]{2,1,0:T(1,128)} %bitcast.25), channel_id=1, replica_groups=mesh['ctx'=64,'vocab'=4] {'ctx'}, dimensions={0}, use_global_device_ids=true | all-gather | bytes 66560 | tf_op jit(solution)/shard_map/all_gather | solution.py:39
  70.8 42.3 %all-gather.1 = f32[64,1,256]{2,1,0:T(1,128)S(1)} all-gather(f32[1,1,256]{2,1,0:T(1,128)} %bitcast.26), channel_id=1, replica_groups=mesh['ctx'=64,'vocab'=4] {'ctx'}, dimensions={0}, use_global_device_ids=true | all-gather | bytes 66560 | tf_op jit(solution)/shard_map/all_gather | solution.py:41
  113.1 42.0 %all-gather = s32[64,1,256]{2,1,0:T(1,128)S(1)} all-gather(s32[1,1,256]{2,1,0:T(1,128)} %bitcast.27), channel_id=1, replica_groups=mesh['ctx'=64,'vocab'=4] {'ctx'}, dimensions={0}, use_global_device_ids=true | all-gather | bytes 66560 | tf_op jit(solution)/shard_map/all_gather | solution.py:40
  155.3 0.6 convert_reduce_fusion
  156.7 6.9 %reshape.82 = bf16[256,8192]{1,0:T(8,128)(2,1)} reshape(bf16[64,4,8192]{2,1,0:T(4,128)(2,1)} %all-gather.7.cloned.1.call-done) | data formatting | bytes 8388608
  163.7 4.8 fusion.14
  168.4 8.5 %pmax.7 = f32[256]{0:T(256)S(1)} all-reduce(f32[256]{0:T(256)S(1)} %fusion.5), channel_id=1, replica_groups=mesh['ctx'=64,'vocab'=4] {'vocab'}, use_global_device_ids=true, to_apply=%region_1.0 | all-reduce | flops 256 | bytes 2048 | tf_op jit(solution)/shard_map/pmax | solution.py:70
  177.0 6.0 %all-reduce.1 = (f32[256]{0:T(256)S(1)}, f32[256]{0:T(256)S(1)}) all-reduce(f32[256]{0:T(256)S(1)} %exponential_multiply_fusion, f32[256]{0:T(256)S(1)} %get-tuple-element.6), channel_id=1, replica_groups=mesh['ctx'=64,'vocab'=4] {'vocab'}, use_global_device_ids=true, to_apply=%region_3.4 | all-reduce | flops 512 | bytes 4096 | tf_op jit(solution)/shard_map/psum | solution.py:71
  183.0 6.7 %fusion.6 = f32[256,8192]{1,0:T(8,128)} fusion(bf16[256,8192]{1,0:T(8,128)(2,1)} %param.9, f32[256,256]{0,1:T(8,128)S(1)} %get-tuple-element.30, f32[]{:T(128)S(6)} %div.16, f32[256]{0:T(256)S(1)} %get-tuple-element.16, f32[256]{0:T(256)S(1)} %add_convert_fusion, s32[256]{0:T(256)S(1)} %add_subtract_fusion), kind=kOutput, calls=%fused_computation.27 | convolution fusion | flops 1074200576 | bytes 12848132 | tf_op jit(solution)/shard_map/dot_general | solution.py:84
  189.8 5.5 %convolution_convert_fusion = bf16[256,8192]{1,0:T(8,128)(2,1)} fusion(bf16[256,8192]{1,0:T(8,128)(2,1)} %reshape.82, f32[256,256]{0,1:T(8,128)S(1)} %get-tuple-element.30, f32[]{:T(128)S(6)} %div.16, f32[256]{0:T(256)S(1)} %get-tuple-element.16, f32[256]{0:T(256)S(1)} %add_convert_fusion, s32[256]{0:T(256)S(1)} %add_subtract_fusion), kind=kOutput, calls=%fused_computation | convolution fusion | flops 1076297728 | bytes 8653828 | tf_op jit(solution)/shard_map/dot_general | solution.py:91
  195.3 0.6 copy-done.3
  195.9 0.6 fusion.3
  197.9 0.6 dynamic-slice
  199.1 46.1 %all-gather.4 = f32[64,1,256]{2,1,0:T(1,128)S(1)} all-gather(f32[1,1,256]{2,1,0:T(1,128)S(1)} %bitcast.24), channel_id=1, replica_groups=mesh['ctx'=64,'vocab'=4] {'ctx'}, dimensions={0}, use_global_device_ids=true | all-gather | bytes 66560 | tf_op jit(solution)/shard_map/all_gather | solution.py:95
  245.3 0.7 reduce_sum.67
  246.1 0.6 pad_maximum_fusion.1
  246.7 147.7 %all-reduce.4.cloned.1.call-done = f32[256,8192]{1,0:T(8,128)} async-done(((f32[256,8192]{1,0:T(8,128)}), f32[256,8192]{1,0:T(8,128)}) %all-reduce.4.cloned.1.call-update) | async-done | bytes 8388624
  394.3 1.6 multiply_reduce_fusion
  397.3 79.0 %psum.23 = f32[]{:T(128)} all-reduce(f32[]{:T(128)} %multiply_reduce_fusion), channel_id=1, replica_groups=mesh['ctx'=64,'vocab'=4] {'ctx','vocab'}, use_global_device_ids=true, to_apply=%region_13.14 | all-reduce | flops 1 | bytes 8 | tf_op jit(solution)/shard_map/psum | solution.py:104
  477.0 1.9 multiply_subtract_fusion
  (29 shorter events, 0.7 us)
Async XLA Ops:
  7.2 149.6 %all-gather.7.cloned.1.call-start = ((), (), s32[]{:S(2)}) async-start(), calls=%async_computation.3 | async-start | bytes 4259840 | tf_op jit(solution)/shard_map/all_gather | solution.py:65
  10.1 146.5 %all-to-all-start = ((f32[64,1,256]{2,1,0:T(1,128)}), f32[64,1,256]{2,1,0:T(1,128)S(1)}, u32[]{:S(2)}, u32[]{:S(2)}) async-start(f32[64,1,256]{2,1,0:T(1,128)} %stack.2), calls=%async_computation | async-start | bytes 131072 | tf_op jit(solution)/shard_map/all_to_all | solution.py:35
  23.3 371.0 %all-reduce.4.cloned.1.call-start = ((), (), s32[]{:S(2)}) async-start(), calls=%async_computation.4 | async-start | bytes 16777216
  189.7 289.1 %reduce-scatter.2.cloned.1.call-start = ((), (), s32[]{:S(2)}) async-start(), calls=%async_computation.2 | async-start | bytes 5242880 | tf_op jit(solution)/shard_map/reduce_scatter | solution.py:92
  195.3 0.7 copy-start.3
  195.3 2.6 copy-start.4
  195.3 281.7 %copy-start = (f32[4,8192]{1,0:T(4,128)S(1)}, f32[4,8192]{1,0:T(4,128)}, u32[]{:S(2)}) copy-start(f32[4,8192]{1,0:T(4,128)} %param.10) | copy-start | bytes 393220
  195.3 281.7 %copy-start.1 = (f32[4,8192]{1,0:T(4,128)S(1)}, f32[4,8192]{1,0:T(4,128)}, u32[]{:S(2)}) copy-start(f32[4,8192]{1,0:T(4,128)} %param.12) | copy-start | bytes 393220
  195.3 281.7 %copy-start.2 = (f32[4,8192]{1,0:T(4,128)S(1)}, f32[4,8192]{1,0:T(4,128)}, u32[]{:S(2)}) copy-start(f32[4,8192]{1,0:T(4,128)} %param.11) | copy-start | bytes 393220
Sparse Core Ops, SparseCore 0:
  11.3 83.4 all-gather.6
  189.9 204.4 all-reduce.3
  397.5 50.3 reduce-scatter.1
